TPU v7x, 256 devices: a whole 4x4x8 slice. The times are simulated.
256 devices in a mesh: slab: 32 (over y, x, z_lo), blk: 8 (over z_hi, core).
Axes of the slice: x: 4, y: 4, z: 8 (z_hi: 4, z_lo: 2; z = z_hi * 2 + z_lo), core: 2. Of those that a mesh axis runs over, the one named last changes fastest.
Arguments:
- interior: float32 [64, 512, 512], P('slab', 'blk'), may hold values from -6 to 6
- sources: float32 [64, 512, 512], P('slab', 'blk'), may hold values from -12 to 12
- absorption: float32 [64, 512, 512], P('slab', 'blk'), may hold values from 0.1 to 4
- bem_panel: bfloat16 [8192, 131072], P('blk', 'slab'), may hold values from -0.03125 to 0.03125
- incident: bfloat16 [131072, 512], P('slab'), may hold values from -160 to 160
- node_cell: int32 [131072], P('slab'), may hold values from 0 to 255
- offset: int32 [1], replicated, may hold values from 0 to 122880, as said below
Outputs:
- relaxed: float32 [64, 512, 512], P('slab', 'blk')
- boundary_flux: float32 [8192, 512], P(('blk', 'slab'))
Inputs may be any that keep to these rules, and one draw needn't show every extreme that they name: offset is a multiple of 8192; rows offset to offset + 8191 lie among the 131072 boundary nodes.
All inputs are finite; a program needn't handle non-finite values.
Results may differ from a plain program's by a relative error of at most 0.0034.
Values sent between devices are 32-bit elements; how exact they have to be, the bound alone decides.
A program may use at most 64 MiB of HBM per device.

v0:
```python
import jax
import jax.numpy as jnp
from jax import lax
from jax.sharding import PartitionSpec as P

SWEEPS = 2
omega = 0.6
center_weight = 8.0 / 3.0


def padded_2(cells, sides, width):
    for axis, dim in sides:
        count = lax.axis_size(axis)
        ends = count - 1
        head = lax.slice_in_dim(cells, 0, width, axis=dim)
        tail = lax.slice_in_dim(cells, cells.shape[dim] - width, cells.shape[dim], axis=dim)
        cells = jnp.concatenate(
            [
                lax.ppermute(tail, axis, [(i, (i + 1) % count) for i in range(ends)]),
                cells,
                lax.ppermute(head, axis, [((i + 1) % count, i) for i in range(ends)]),
            ],
            axis=dim,
        )
    return cells


def stiffness(padded):
    along_x = padded[:, :, :-2] + padded[:, :, 2:]
    middle = padded[:, :, 1:-1]
    plus_mid = along_x + middle
    plane_sum = plus_mid[:, :-2] + plus_mid[:, 1:-1] + plus_mid[:, 2:]
    total_sum = plane_sum[:-2] + plane_sum[1:-1] + plane_sum[2:]
    cross_xy = along_x[:, :-2] + along_x[:, 2:]
    corner_sum = cross_xy[:-2] + cross_xy[2:]
    face_sum = (
        along_x[1:-1, 1:-1]
        + middle[1:-1, :-2]
        + middle[1:-1, 2:]
        + middle[:-2, 1:-1]
        + middle[2:, 1:-1]
    )
    center = middle[1:-1, 1:-1]
    edge_sum = total_sum - center - face_sum - corner_sum
    return center_weight * center - edge_sum / 6.0 - corner_sum / 12.0


def sweep_once(padded, sources, absorption):
    center = padded[1:-1, 1:-1, 1:-1]
    applied = stiffness(padded) + absorption * center
    return center + omega * (sources - applied) / (center_weight + absorption)


def pad_x(values):
    return jnp.pad(values, ((0, 0), (0, 0), (1, 1)))


def per_device(interior, sources, absorption, bem_panel, incident, node_cell, offset):
    depth_z, depth_y, width_x = interior.shape
    current = interior
    for sweep_idx in range(SWEEPS):
        padded = padded_2(current, (("slab", 0), ("blk", 1)), 1)
        current = sweep_once(pad_x(padded), sources, absorption)
    slab_cols = incident.shape[0]
    own_count = slab_cols // lax.axis_size("blk")
    x_faces = jnp.stack([interior[:, :, 0], interior[:, :, width_x - 1]], axis=-1).reshape(-1)
    own_cells = lax.dynamic_slice_in_dim(node_cell, lax.axis_index("blk") * own_count, own_count, 0)
    own_trace = jnp.take(x_faces, own_cells, axis=0)
    trace = lax.all_gather(own_trace, "blk", axis=0, tiled=True)
    fields = (incident.astype(jnp.float32) + trace[:, None]).astype(jnp.bfloat16)
    wide = fields.astype(jnp.float32)
    node_total = slab_cols * lax.axis_size("slab")
    squares = lax.psum(jnp.sum(wide * wide, axis=0), "slab")
    norms = jnp.sqrt(squares / node_total + 1e-06)
    panel_rows = bem_panel.shape[0]
    first_col = lax.axis_index("slab") * slab_cols
    shift_rows = offset[0] + lax.axis_index("blk") * panel_rows - first_col
    share = panel_rows // lax.axis_size("slab")
    product = jnp.dot(bem_panel, fields, preferred_element_type=jnp.float32)
    node_pos = shift_rows + jnp.arange(panel_rows, dtype=jnp.int32)
    valid = (node_pos >= 0) & (node_pos < slab_cols)
    picked = jnp.take(wide, jnp.clip(node_pos, 0, slab_cols - 1), axis=0)
    summed = product + 0.5 * jnp.where(valid[:, None], picked, 0.0)
    summed = summed / norms[None, :]
    summed_all = lax.psum(summed, "slab")
    owned = lax.dynamic_slice_in_dim(summed_all, lax.axis_index("slab") * share, share, 0)
    return (current, owned)


def solution(mesh):
    in_specs = (
        P("slab", "blk", None),
        P("slab", "blk", None),
        P("slab", "blk", None),
        P("blk", "slab"),
        P("slab", None),
        P("slab"),
        P(),
    )
    out_specs = (P("slab", "blk", None), P(("blk", "slab"), None))
    return jax.shard_map(
        per_device, mesh=mesh, in_specs=in_specs, out_specs=out_specs, check_vma=False
    )
```

profile of v0, /device:TPU:32, one launch (start us, length us, event | category | flops | bytes accessed | tf_op | source)
XLA Modules:
  0.0 480.4 jit_solution(14701295206737365730)
XLA Ops:
  7.2 0.0 all-reduce.4.cloned.1.call-start
  7.2 1.0 fusion.47
  8.2 2.9 collective-permute-start
  11.2 2.9 collective-permute-start.1
  14.1 1.0 fusion.45
  15.7 0.1 copy.18
  15.8 0.1 copy.19
  15.9 0.1 copy.15
  16.0 0.1 reshape.43
  16.1 0.8 compare_select_fusion.2
  16.9 3.5 gather_fusion
  20.4 0.8 and_select_fusion
  21.2 17.4 %all-gather = f32[8,1,512]{2,1,0:T(1,128)S(1)} all-gather(f32[1,1,512]{2,1,0:T(1,128)S(1)} %bitcast.13), channel_id=1, replica_groups=mesh['slab'=32,'blk'=8] {'blk'}, dimensions={0}, use_global_device_ids=true | all-gather | bytes 18432 | tf_op jit(solution)/shard_map/all_gather | solution.py:69
  38.6 5.4 %multiply_reduce_fusion = (f32[512]{0:T(512)S(1)}, f32[4096,512]{1,0:T(8,128)}) fusion(f32[4096]{0:T(1024)S(1)} %bitcast.10, bf16[4096,512]{1,0:T(8,128)(2,1)} %param.11), kind=kLoop, calls=%fused_computation.2 | loop fusion | flops 12582400 | bytes 12601344 | tf_op jit(solution)/shard_map/reduce_sum | solution.py:73
  44.0 79.4 %psum.14 = f32[512]{0:T(512)S(1)} all-reduce(f32[512]{0:T(512)S(1)} %get-tuple-element.12), channel_id=1, replica_groups=mesh['slab'=32,'blk'=8] {'slab'}, use_global_device_ids=true, to_apply=%region_1.2 | all-reduce | flops 512 | bytes 4096 | tf_op jit(solution)/shard_map/psum | solution.py:73
  123.4 7.4 %gather_fusion.1 = f32[1024,512]{1,0:T(8,128)S(1)} fusion(f32[4096,512]{1,0:T(8,128)} %get-tuple-element.13, s32[1024]{0:T(1024)S(1)} %get-tuple-element.27), kind=kCustom, calls=%fused_computation.1 | custom fusion | bytes 4198400 | tf_op jit(solution)/shard_map/jit(_take)/gather | solution.py:82
  130.9 0.0 copy-start
  130.9 1.9 copy.16
  132.7 0.0 collective-permute-done
  132.8 0.0 collective-permute-done.1
  132.9 1.3 collective-permute-start.2
  134.2 1.3 collective-permute-start.3
  135.5 11.9 %fusion = f32[1024,512]{0,1:T(8,128)} fusion(f32[1024,512]{0,1:T(8,128)} %copy.16, bf16[1024,4096]{1,0:T(8,128)(2,1)} %param.10, f32[512]{0:T(512)S(1)} %add_sqrt_fusion, pred[1024]{0:T(1024)(128)(4,1)S(1)} %get-tuple-element.28, pred[1024]{0:T(1024)(128)(4,1)S(1)} %get-tuple-element.29, bf16[4096,512]{1,0:T(8,128)(2,1)} %param.11, f32[4096]{0:T(1024)S(1)} %bitcast.11), kind=kOutput, calls=%fused_computation.5 | convolution fusion | flops 4303880192 | bytes 16797696 | tf_op jit(solution)/shard_map/dot_general | solution.py:79
  147.4 0.0 all-reduce.4.cloned.1.call-update
  147.4 0.0 collective-permute-done.2
  147.4 0.0 collective-permute-done.3
  147.5 0.1 pad_maximum_fusion
  147.5 0.4 fusion.39
  147.9 0.2 slice_add_fusion.3
  148.1 0.2 copy-done.1
  148.4 0.1 copy-done.2
  148.4 0.3 fusion.28
  148.8 2.9 collective-permute-start.4
  151.7 4.7 collective-permute-start.5
  156.4 1.5 collective-permute-done.4
  157.9 2.7 collective-permute-done.5
  160.6 2.1 collective-permute-start.6
  162.7 1.3 collective-permute-start.7
  164.0 0.0 collective-permute-done.6
  164.0 4.8 collective-permute-done.7
  168.7 0.1 pad_maximum_fusion.1
  168.8 0.4 fusion.40
  169.2 0.1 slice_add_fusion
  169.3 0.1 slice_add_fusion.1
  169.4 1.0 fusion.13
  170.4 301.3 %all-reduce.4.cloned.1.call-done = f32[1024,512]{0,1:T(8,128)} async-done(((f32[1024,512]{0,1:T(8,128)}), f32[1024,512]{0,1:T(8,128)}) %all-reduce.4.cloned.1.call-update) | async-done | bytes 2097168 | tf_op jit(solution)/shard_map/psum | solution.py:85
  471.7 1.1 constant_dynamic-slice_fusion
  472.8 0.7 copy.17
  (14 shorter events, 0.2 us)
Async XLA Ops:
  7.2 464.6 %all-reduce.4.cloned.1.call-start = ((), (), s32[]{:S(2)}) async-start(), calls=%async_computation | async-start | bytes 4194304 | tf_op jit(solution)/shard_map/psum | solution.py:85
  8.2 124.5 %collective-permute-start = (f32[1,64,512]{2,1,0:T(8,128)S(1)}, f32[1,64,512]{2,1,0:T(8,128)S(1)}, u32[]{:S(2)}, u32[]{:S(2)}) collective-permute-start(f32[1,64,512]{2,1,0:T(8,128)S(1)} %get-tuple-element.22), channel_id=1, source_target_pairs={{0,8},{8,16},{16,24},{24,32},{32,40},{40,48},{48,56},{56,64},{64,7... | collective-permute-start | bytes 393224 | tf_op jit(solution)/shard_map/ppermute | solution.py:19
  11.2 121.7 %collective-permute-start.1 = (f32[1,64,512]{2,1,0:T(8,128)S(1)}, f32[1,64,512]{2,1,0:T(8,128)S(1)}, u32[]{:S(2)}, u32[]{:S(2)}) collective-permute-start(f32[1,64,512]{2,1,0:T(8,128)S(1)} %get-tuple-element.23), channel_id=1, source_target_pairs={{8,0},{16,8},{24,16},{32,24},{40,32},{48,40},{56,48},{64,56},{72,6... | collective-permute-start | bytes 393224 | tf_op jit(solution)/shard_map/ppermute | solution.py:21
  130.9 1.9 copy-start
  132.9 14.6 %collective-permute-start.2 = (f32[4,1,512]{2,1,0:T(1,128)S(1)}, f32[4,1,512]{2,1,0:T(1,128)S(1)}, u32[]{:S(2)}, u32[]{:S(2)}) collective-permute-start(f32[4,1,512]{2,1,0:T(1,128)S(1)} %get-tuple-element.16), channel_id=1, source_target_pairs={{0,1},{1,2},{2,3},{3,4},{4,5},{5,6},{6,7},{8,9},{9,10},{10,11},{11... | collective-permute-start | bytes 24584 | tf_op jit(solution)/shard_map/ppermute | solution.py:19
  134.2 13.3 %collective-permute-start.3 = (f32[4,1,512]{2,1,0:T(1,128)S(1)}, f32[4,1,512]{2,1,0:T(1,128)S(1)}, u32[]{:S(2)}, u32[]{:S(2)}) collective-permute-start(f32[4,1,512]{2,1,0:T(1,128)S(1)} %get-tuple-element.17), channel_id=1, source_target_pairs={{1,0},{2,1},{3,2},{4,3},{5,4},{6,5},{7,6},{9,8},{10,9},{11,10},{12... | collective-permute-start | bytes 24584 | tf_op jit(solution)/shard_map/ppermute | solution.py:21
  147.4 0.9 copy-start.1
  147.4 1.0 copy-start.2
  148.8 9.1 %collective-permute-start.4 = (f32[1,64,512]{2,1,0:T(8,128)S(1)}, f32[1,64,512]{2,1,0:T(8,128)S(1)}, u32[]{:S(2)}, u32[]{:S(2)}) collective-permute-start(f32[1,64,512]{2,1,0:T(8,128)S(1)} %get-tuple-element.20), channel_id=1, source_target_pairs={{0,8},{8,16},{16,24},{24,32},{32,40},{40,48},{48,56},{56,64},{64,7... | collective-permute-start | bytes 393224 | tf_op jit(solution)/shard_map/ppermute | solution.py:19
  151.7 8.8 %collective-permute-start.5 = (f32[1,64,512]{2,1,0:T(8,128)S(1)}, f32[1,64,512]{2,1,0:T(8,128)S(1)}, u32[]{:S(2)}, u32[]{:S(2)}) collective-permute-start(f32[1,64,512]{2,1,0:T(8,128)S(1)} %get-tuple-element.21), channel_id=1, source_target_pairs={{8,0},{16,8},{24,16},{32,24},{40,32},{48,40},{56,48},{64,56},{72,6... | collective-permute-start | bytes 393224 | tf_op jit(solution)/shard_map/ppermute | solution.py:21
  160.6 3.4 collective-permute-start.6
  162.7 6.1 %collective-permute-start.7 = (f32[4,1,512]{2,1,0:T(1,128)S(1)}, f32[4,1,512]{2,1,0:T(1,128)S(1)}, u32[]{:S(2)}, u32[]{:S(2)}) collective-permute-start(f32[4,1,512]{2,1,0:T(1,128)S(1)} %get-tuple-element.15), channel_id=1, source_target_pairs={{1,0},{2,1},{3,2},{4,3},{5,4},{6,5},{7,6},{9,8},{10,9},{11,10},{12... | collective-permute-start | bytes 24584 | tf_op jit(solution)/shard_map/ppermute | solution.py:21
Sparse Core Ops, SparseCore 0:
  147.6 324.1 all-reduce.3
where the time goes:
time: 481 us; the launch traced here: 480 us
  waiting for transfers between devices  310 us (64%)
  blocking collectives  96.8 us (20%)
  starting transfers between devices  19.4 us (4%)
  local copies, waits for them, and re-layouts  17.3 us (4%)
  between operations  15 us (3%)
  matrix products  11.9 us (2%)
  other arithmetic  9.66 us (2%)
    psum x1, waiting for transfers between devices, per_device(): summed_all = lax.psum(summed, 'slab')  301 us
    psum x1, blocking collectives, per_device(): squares = lax.psum(jnp.sum(wide * wide, axis=0), 'slab')  79.4 us
    all_gather x1, blocking collectives, per_device(): trace = lax.all_gather(own_trace, 'blk', axis=0, tiled=True)  17.4 us
    dot_general x1, matrix products, per_device(): product = jnp.dot(bem_panel, fields, preferred_element_type=jnp.float32)  11.9 us
    ppermute x4, starting transfers between devices, padded_2(): lax.ppermute(head, axis, [((i + 1) % count, i) for i in range(ends)])  10.1 us
  transfers between devices with their start and end apart: 9, of which 4 were waited for; matrix products, arithmetic and copies ran while one was open for 7% of the time, Pallas kernels for 0%

commit v1 on v0

--- a/solution.py
+++ b/solution.py
@@ -66,7 +66,10 @@
     x_faces = jnp.stack([interior[:, :, 0], interior[:, :, width_x - 1]], axis=-1).reshape(-1)
     own_cells = lax.dynamic_slice_in_dim(node_cell, lax.axis_index("blk") * own_count, own_count, 0)
     own_trace = jnp.take(x_faces, own_cells, axis=0)
-    trace = lax.all_gather(own_trace, "blk", axis=0, tiled=True)
+    size = lax.axis_size("blk")
+    blocks = jnp.stack([own_trace for _ in range(size)])
+    blocks = lax.all_to_all(blocks, "blk", split_axis=0, concat_axis=0)
+    trace = jnp.concatenate(blocks, axis=0)
     fields = (incident.astype(jnp.float32) + trace[:, None]).astype(jnp.bfloat16)
     wide = fields.astype(jnp.float32)
     node_total = slab_cols * lax.axis_size("slab")

time: 481 us -> 475 us (0.988)
  blocking collectives: 96.8 us -> 78.5 us
  starting transfers between devices: 19.4 us -> 29.6 us
    all_gather x1 -> x0, blocking collectives: 17.4 us -> none  [per_device(): trace = lax.all_gather(own_trace, 'blk', axis=0, tiled=True)]
    all_to_all x0 -> x1, starting transfers between devices: none -> 7.57 us  [per_device(): blocks = lax.all_to_all(blocks, 'blk', split_axis=0, concat_axis=0)]
  transfers between devices with their start and end apart: 9 -> 10, of which waited for: 4 -> 5; matrix products, arithmetic and copies ran while one was open for 7% -> 6% of each run, Pallas kernels for 0% -> 0%
where the time goes in v1:
time: 475 us
  waiting for transfers between devices  312 us (66%)
  blocking collectives  78.5 us (17%)
  starting transfers between devices  29.6 us (6%)
  local copies, waits for them, and re-layouts  17.9 us (4%)
  between operations  15 us (3%)
  matrix products  11.9 us (3%)
  other arithmetic  9.67 us (2%)
    psum x1, waiting for transfers between devices, per_device(): summed_all = lax.psum(summed, 'slab')  302 us
    psum x1, blocking collectives, per_device(): squares = lax.psum(jnp.sum(wide * wide, axis=0), 'slab')  78.5 us
    ppermute x4, starting transfers between devices, padded_2(): lax.ppermute(tail, axis, [(i, (i + 1) % count) for i in range(ends)])  12.8 us
    dot_general x1, matrix products, per_device(): product = jnp.dot(bem_panel, fields, preferred_element_type=jnp.float32)  11.9 us
  transfers between devices with their start and end apart: 10, of which 5 were waited for; matrix products, arithmetic and copies ran while one was open for 6% of the time, Pallas kernels for 0%

profile of v1, /device:TPU:32, one launch (start us, length us, event | category | flops | bytes accessed | tf_op | source)
XLA Modules:
  0.0 474.8 jit_solution(15005128021981897233)
XLA Ops:
  7.8 1.0 fusion.45
  8.8 0.1 copy.18
  8.9 0.1 copy.19
  9.0 0.1 copy.15
  9.1 0.1 reshape.52
  9.2 0.8 compare_select_fusion.2
  10.0 3.5 gather_fusion
  13.5 0.8 and_select_fusion
  14.3 0.6 stack.5
  14.9 7.6 %all-to-all-start = ((f32[8,1,512]{2,1,0:T(1,128)}), f32[8,1,512]{2,1,0:T(1,128)S(1)}, u32[]{:S(2)}, u32[]{:S(2)}) async-start(f32[8,1,512]{2,1,0:T(1,128)} %stack.5), calls=%async_computation | async-start | bytes 32768 | tf_op jit(solution)/shard_map/all_to_all | solution.py:71
  22.5 0.0 all-reduce.4.cloned.1.call-start
  22.5 1.0 fusion.47
  23.5 3.8 collective-permute-start
  27.4 2.0 collective-permute-start.1
  29.4 0.9 all-to-all-done
  30.3 5.4 %multiply_reduce_fusion = (f32[512]{0:T(512)S(1)}, f32[4096,512]{1,0:T(8,128)}) fusion(f32[4096]{0:T(1024)S(1)} %bitcast.9, bf16[4096,512]{1,0:T(8,128)(2,1)} %param.11), kind=kLoop, calls=%fused_computation.2 | loop fusion | flops 12582400 | bytes 12601344 | tf_op jit(solution)/shard_map/reduce_sum | solution.py:76
  35.7 7.4 %gather_fusion.1 = f32[1024,512]{1,0:T(8,128)S(1)} fusion(f32[4096,512]{1,0:T(8,128)} %get-tuple-element.13, s32[1024]{0:T(1024)S(1)} %get-tuple-element.27), kind=kCustom, calls=%fused_computation.1 | custom fusion | bytes 4198400 | tf_op jit(solution)/shard_map/jit(_take)/gather | solution.py:85
  43.1 0.0 copy-start
  43.1 1.8 copy.16
  45.0 78.5 %psum.14 = f32[512]{0:T(512)S(1)} all-reduce(f32[512]{0:T(512)S(1)} %get-tuple-element.12), channel_id=1, replica_groups=mesh['slab'=32,'blk'=8] {'slab'}, use_global_device_ids=true, to_apply=%region_1.2 | all-reduce | flops 512 | bytes 4096 | tf_op jit(solution)/shard_map/psum | solution.py:76
  123.5 0.0 collective-permute-done
  123.6 0.0 collective-permute-done.1
  123.7 1.3 collective-permute-start.2
  125.0 1.3 collective-permute-start.3
  126.3 11.9 %fusion = f32[1024,512]{0,1:T(8,128)} fusion(f32[1024,512]{0,1:T(8,128)} %copy.16, bf16[1024,4096]{1,0:T(8,128)(2,1)} %param.10, f32[512]{0:T(512)S(1)} %add_sqrt_fusion, pred[1024]{0:T(1024)(128)(4,1)S(1)} %get-tuple-element.28, pred[1024]{0:T(1024)(128)(4,1)S(1)} %get-tuple-element.29, bf16[4096,512]{1,0:T(8,128)(2,1)} %param.11, f32[4096]{0:T(1024)S(1)} %bitcast.10), kind=kOutput, calls=%fused_computation.5 | convolution fusion | flops 4303880192 | bytes 16797696 | tf_op jit(solution)/shard_map/dot_general | solution.py:82
  138.2 0.0 all-reduce.4.cloned.1.call-update
  138.2 0.0 collective-permute-done.2
  138.2 0.1 pad_maximum_fusion
  138.3 0.4 fusion.39
  138.7 0.2 slice_add_fusion.3
  138.9 0.2 copy-done.1
  139.1 0.1 copy-done.2
  139.2 0.3 fusion.28
  139.6 3.8 collective-permute-start.4
  143.4 4.7 collective-permute-start.5
  148.1 1.0 collective-permute-done.4
  149.1 2.1 collective-permute-done.5
  151.2 3.8 collective-permute-start.6
  155.0 1.3 collective-permute-start.7
  156.3 6.5 %collective-permute-done.7 = f32[4,1,512]{2,1,0:T(1,128)S(1)} collective-permute-done((f32[4,1,512]{2,1,0:T(1,128)S(1)}, f32[4,1,512]{2,1,0:T(1,128)S(1)}, u32[]{:S(2)}, u32[]{:S(2)}) %collective-permute-start.7) | collective-permute-done | bytes 8224 | tf_op jit(solution)/shard_map/ppermute | solution.py:21
  162.9 0.1 pad_maximum_fusion.1
  162.9 0.4 fusion.40
  163.3 0.1 slice_add_fusion
  163.4 0.1 slice_add_fusion.1
  163.5 1.0 fusion.13
  164.5 301.6 %all-reduce.4.cloned.1.call-done = f32[1024,512]{0,1:T(8,128)} async-done(((f32[1024,512]{0,1:T(8,128)}), f32[1024,512]{0,1:T(8,128)}) %all-reduce.4.cloned.1.call-update) | async-done | bytes 2097168 | tf_op jit(solution)/shard_map/psum | solution.py:88
  466.2 1.1 constant_dynamic-slice_fusion
  467.3 0.7 copy.17
  (16 shorter events, 0.2 us)
Async XLA Ops:
  14.9 15.4 %all-to-all-start = ((f32[8,1,512]{2,1,0:T(1,128)}), f32[8,1,512]{2,1,0:T(1,128)S(1)}, u32[]{:S(2)}, u32[]{:S(2)}) async-start(f32[8,1,512]{2,1,0:T(1,128)} %stack.5), calls=%async_computation | async-start | bytes 32768 | tf_op jit(solution)/shard_map/all_to_all | solution.py:71
  22.5 443.7 %all-reduce.4.cloned.1.call-start = ((), (), s32[]{:S(2)}) async-start(), calls=%async_computation.1 | async-start | bytes 4194304 | tf_op jit(solution)/shard_map/psum | solution.py:88
  23.5 100.0 %collective-permute-start = (f32[1,64,512]{2,1,0:T(8,128)S(1)}, f32[1,64,512]{2,1,0:T(8,128)S(1)}, u32[]{:S(2)}, u32[]{:S(2)}) collective-permute-start(f32[1,64,512]{2,1,0:T(8,128)S(1)} %get-tuple-element.22), channel_id=1, source_target_pairs={{0,8},{8,16},{16,24},{24,32},{32,40},{40,48},{48,56},{56,64},{64,7... | collective-permute-start | bytes 393224 | tf_op jit(solution)/shard_map/ppermute | solution.py:19
  27.4 96.2 %collective-permute-start.1 = (f32[1,64,512]{2,1,0:T(8,128)S(1)}, f32[1,64,512]{2,1,0:T(8,128)S(1)}, u32[]{:S(2)}, u32[]{:S(2)}) collective-permute-start(f32[1,64,512]{2,1,0:T(8,128)S(1)} %get-tuple-element.23), channel_id=1, source_target_pairs={{8,0},{16,8},{24,16},{32,24},{40,32},{48,40},{56,48},{64,56},{72,6... | collective-permute-start | bytes 393224 | tf_op jit(solution)/shard_map/ppermute | solution.py:21
  43.1 80.4 %copy-start = (f32[2,64,512]{2,1,0:T(8,128)S(1)}, f32[2,64,512]{2,1,0:T(8,128)}, u32[]{:S(2)}) copy-start(f32[2,64,512]{2,1,0:T(8,128)} %param.7) | copy-start | bytes 786436
  123.7 14.6 %collective-permute-start.2 = (f32[4,1,512]{2,1,0:T(1,128)S(1)}, f32[4,1,512]{2,1,0:T(1,128)S(1)}, u32[]{:S(2)}, u32[]{:S(2)}) collective-permute-start(f32[4,1,512]{2,1,0:T(1,128)S(1)} %get-tuple-element.16), channel_id=1, source_target_pairs={{0,1},{1,2},{2,3},{3,4},{4,5},{5,6},{6,7},{8,9},{9,10},{10,11},{11... | collective-permute-start | bytes 24584 | tf_op jit(solution)/shard_map/ppermute | solution.py:19
  125.0 13.3 %collective-permute-start.3 = (f32[4,1,512]{2,1,0:T(1,128)S(1)}, f32[4,1,512]{2,1,0:T(1,128)S(1)}, u32[]{:S(2)}, u32[]{:S(2)}) collective-permute-start(f32[4,1,512]{2,1,0:T(1,128)S(1)} %get-tuple-element.17), channel_id=1, source_target_pairs={{1,0},{2,1},{3,2},{4,3},{5,4},{6,5},{7,6},{9,8},{10,9},{11,10},{12... | collective-permute-start | bytes 24584 | tf_op jit(solution)/shard_map/ppermute | solution.py:21
  138.2 0.9 copy-start.1
  138.2 1.0 copy-start.2
  139.6 9.5 %collective-permute-start.4 = (f32[1,64,512]{2,1,0:T(8,128)S(1)}, f32[1,64,512]{2,1,0:T(8,128)S(1)}, u32[]{:S(2)}, u32[]{:S(2)}) collective-permute-start(f32[1,64,512]{2,1,0:T(8,128)S(1)} %get-tuple-element.20), channel_id=1, source_target_pairs={{0,8},{8,16},{16,24},{24,32},{32,40},{40,48},{48,56},{56,64},{64,7... | collective-permute-start | bytes 393224 | tf_op jit(solution)/shard_map/ppermute | solution.py:19
  143.4 7.8 %collective-permute-start.5 = (f32[1,64,512]{2,1,0:T(8,128)S(1)}, f32[1,64,512]{2,1,0:T(8,128)S(1)}, u32[]{:S(2)}, u32[]{:S(2)}) collective-permute-start(f32[1,64,512]{2,1,0:T(8,128)S(1)} %get-tuple-element.21), channel_id=1, source_target_pairs={{8,0},{16,8},{24,16},{32,24},{40,32},{48,40},{56,48},{64,56},{72,6... | collective-permute-start | bytes 393224 | tf_op jit(solution)/shard_map/ppermute | solution.py:21
  151.2 5.2 %collective-permute-start.6 = (f32[4,1,512]{2,1,0:T(1,128)S(1)}, f32[4,1,512]{2,1,0:T(1,128)S(1)}, u32[]{:S(2)}, u32[]{:S(2)}) collective-permute-start(f32[4,1,512]{2,1,0:T(1,128)S(1)} %get-tuple-element.14), channel_id=1, source_target_pairs={{0,1},{1,2},{2,3},{3,4},{4,5},{5,6},{6,7},{8,9},{9,10},{10,11},{11... | collective-permute-start | bytes 24584 | tf_op jit(solution)/shard_map/ppermute | solution.py:19
  155.0 7.8 %collective-permute-start.7 = (f32[4,1,512]{2,1,0:T(1,128)S(1)}, f32[4,1,512]{2,1,0:T(1,128)S(1)}, u32[]{:S(2)}, u32[]{:S(2)}) collective-permute-start(f32[4,1,512]{2,1,0:T(1,128)S(1)} %get-tuple-element.15), channel_id=1, source_target_pairs={{1,0},{2,1},{3,2},{4,3},{5,4},{6,5},{7,6},{9,8},{10,9},{11,10},{12... | collective-permute-start | bytes 24584 | tf_op jit(solution)/shard_map/ppermute | solution.py:21
Sparse Core Ops, SparseCore 0:
  138.3 327.7 all-reduce.3
